TPU v7x, 32 devices: a whole 2x2x4 slice. The times are simulated.
32 devices in a mesh: ctx: 16 (over z, x, core), fsdp: 2 (over y).
Axes of the slice: x: 2, y: 2, z: 4, core: 2. Of those that a mesh axis runs over, the one named last changes fastest.
Arguments:
- hidden_in: bfloat16 [2, 2048, 1024], P('fsdp', 'ctx'), may hold values from -6 to 6
- doc_lengths: int32 [2, 8], P('fsdp'), may hold values from 1 to 1920, as said below
- attn_gain: float32 [1024], replicated, may hold values from 0.5 to 1.5
- query_gain: float32 [64], replicated, may hold values from 0.5 to 1.5
- key_norm_gain: float32 [64], replicated, may hold values from 0.5 to 1.5
- ffn_gain: float32 [1024], replicated, may hold values from 0.5 to 1.5
- query_proj: float32 [1024, 1024], P('fsdp'), may hold values from -0.1875 to 0.1875
- key_weight: float32 [1024, 512], P('fsdp'), may hold values from -0.1875 to 0.1875
- value_weight: float32 [1024, 512], P('fsdp'), may hold values from -0.1875 to 0.1875
- attn_proj: float32 [1024, 1024], P('fsdp'), may hold values from -3 to 3
- gate_proj: float32 [1024, 4608], P('fsdp'), may hold values from -0.1875 to 0.1875
- up_proj: float32 [1024, 4608], P('fsdp'), may hold values from -0.1875 to 0.1875
- down_proj: float32 [4608, 1024], P('fsdp'), may hold values from -0.09375 to 0.09375
- out_cotangent: bfloat16 [2, 2048, 1024], P('fsdp', 'ctx'), may hold values from -6 to 6
Outputs:
- hidden_out: float32 [2, 2048, 1024], P('fsdp', 'ctx')
- input_grad: float32 [2, 2048, 1024], P('fsdp', 'ctx')
- attn_gain_grad: float32 [1024], replicated
- query_gain_grad: float32 [64], replicated
- key_gain_grad: float32 [64], replicated
- ffn_gain_grad: float32 [1024], replicated
- query_grad: float32 [1024, 1024], P('fsdp', 'ctx')
- key_grad: float32 [1024, 512], P('fsdp', 'ctx')
- value_grad: float32 [1024, 512], P('fsdp', 'ctx')
- attn_grad: float32 [1024, 1024], P('fsdp', 'ctx')
- gate_grad: float32 [1024, 4608], P('fsdp', 'ctx')
- up_grad: float32 [1024, 4608], P('fsdp', 'ctx')
- down_grad: float32 [4608, 1024], P('fsdp', 'ctx')
Inputs may be any that keep to these rules, and one draw needn't show every extreme that they name: `doc_lengths`: each stream's 8 document lengths sum to 2048; in every stream exactly one document has 1920 tokens, and it is neither the first nor the last of its stream.
All inputs are finite; a program needn't handle non-finite values.
Results may differ from a plain program's by a relative error of at most 0.014.
Values may be sent and summed in bfloat16 or wider, within the bound.
A program may use at most 320 MiB of HBM per device.

v0:
```python
import functools
import math

import jax
import jax.numpy as jnp
from jax import lax
from jax.experimental import pallas as pl
from jax.experimental.pallas import tpu as pltpu
from jax.sharding import PartitionSpec as P

QUERY_HEADS = 16
KEY_VALUE_HEADS = 8
HEAD_SIZE = 64
FF = 4608
WIDTH = 1024
ROWS = 128

epsilon = 1e-05
rope_base = 1000000.0
MESH = pl.DeviceIdType.MESH
ANY = pl.ANY
VMEM_LIMIT = 64 * 2**20 - 2**17
bf16 = jnp.bfloat16
f32 = jnp.float32


def who():
    n = lax.axis_size("ctx")
    c = lax.axis_index("ctx")
    f = lax.axis_index("fsdp")
    q = n // 4
    return c // q, (c % q) // 2, c % 2, f


def dev(z, m, core, f):
    return (z * (lax.axis_size("ctx") // 4) + m * 2 + core, f)


def slot(z, core):
    return z * 2 + core


def enter(peers):
    bar = pltpu.get_barrier_semaphore()
    for p in peers:
        pl.semaphore_signal(bar, inc=1, device_id=p, device_id_type=MESH)
    pl.semaphore_wait(bar, len(peers))


def rcopy(src, dst, s, r, to):
    return pltpu.make_async_remote_copy(
        src_ref=src, dst_ref=dst, send_sem=s, recv_sem=r, device_id=to, device_id_type=MESH
    )


def comm_params(cid):
    return pltpu.CompilerParams(collective_id=cid, has_side_effects=True)


def any_specs(n):
    return [pl.BlockSpec(memory_space=ANY)] * n


def line_of(z):
    return z + 1 - 2 * (z % 2), 2 - z // 2, 3 - 3 * (z // 2), 1 - ((z + 1) // 2) % 2


class Gather:
    def __init__(self, src, dst, ss, rs):
        z, m, core, f = who()
        partner, middle, end, self.at_end = line_of(z)
        self.src, self.dst, self.ss, self.rs = src, dst, ss, rs
        self.me = slot(z, core)
        self.slots = [slot(zz, core) for zz in (partner, middle, end)]
        self.partner = dev(partner, m, core, f)
        self.middle = dev(middle, m, core, f)
        self.sib = dev(z, m, 1 - core, f)

    def copy(self, k):
        src, dst, ss, rs = self.src, self.dst, self.ss.at[k], self.rs
        if k == 0:
            return rcopy(src, dst.at[self.me], ss, rs.at[0], self.partner)
        if k == 1:
            return rcopy(src, dst.at[self.me], ss, rs.at[1 + self.at_end], self.middle)
        if k == 3:
            return rcopy(src, dst.at[self.me], ss, rs.at[3], self.sib)
        if k < 7:
            j = self.slots[k - 4]
            return rcopy(dst.at[j], dst.at[j], ss, rs.at[k], self.sib)
        j = self.slots[k - 6]
        return rcopy(dst.at[j], dst.at[j], ss, rs.at[k - 6], self.partner)

    def own(self):
        for k in (1, 0, 3):
            self.copy(k).start()

    def take(self, kind):
        j = self.slots[kind]
        rcopy(
            self.dst.at[j], self.dst.at[j], self.ss.at[0], self.rs.at[kind], self.partner
        ).wait_recv()
        if kind > 0:

            @pl.when(self.at_end == 0)
            def _():
                self.copy(6 + kind).start()

        self.copy(4 + kind).start()

    def rest(self):
        for k in range(3, 7):
            self.copy(k).wait_recv()

    def sent(self):
        for k in (0, 1, 3, 4, 5, 6):
            self.copy(k).wait_send()

        @pl.when(self.at_end == 0)
        def _():
            self.copy(7).wait_send()
            self.copy(8).wait_send()


class Scatter:
    def __init__(self, part, buf, sums, relay, rx, ss, rs):
        z, m, self.core, f = who()
        core = self.core
        partner, middle, end, self.at_end = line_of(z)
        self.z = z
        self.part, self.buf, self.sums, self.relay_buf, self.rx = part, buf, sums, relay, rx
        self.ss, self.rs = ss, rs
        self.order = [end, middle, partner, z]
        self.sib = dev(z, m, 1 - core, f)
        self.to = [dev(zz, m, core, f) for zz in self.order[:3]]

    def sibling(self, i):
        return rcopy(
            self.part.at[self.order[i], 1 - self.core],
            self.buf.at[i],
            self.ss.at[i],
            self.rs.at[i],
            self.sib,
        )

    def copy(self, i, at_end):
        if i == 2:
            return rcopy(
                self.sums.at[2], self.rx.at[0], self.ss.at[6], self.rs.at[4], self.to[2]
            )
        if at_end:
            return rcopy(
                self.sums.at[i], self.relay_buf.at[i], self.ss.at[4 + i], self.rs.at[6 + i], self.to[2]
            )
        return rcopy(self.sums.at[i], self.rx.at[1], self.ss.at[4 + i], self.rs.at[5], self.to[i])

    def pass_on(self, i):
        self.sibling(i).wait_recv()
        self.sums[i] = (
            self.part[self.order[i], self.core].astype(f32) + self.buf[i].astype(f32)
        ).astype(bf16)
        if i == 2:
            self.copy(2, True).start()
        else:

            @pl.when(self.at_end == 1)
            def _():
                self.copy(i, True).start()

    def relay(self, i):
        @pl.when(self.at_end == 0)
        def _():
            self.copy(i, True).wait_recv()
            self.sums[i] = (
                self.sums[i].astype(f32) + self.relay_buf[i].astype(f32)
            ).astype(bf16)
            self.copy(i, False).start()

    def total(self):
        self.sibling(3).wait_recv()
        total = self.part[self.z, self.core].astype(f32) + self.buf[3].astype(f32)
        self.copy(2, True).wait_recv()
        total = total + self.rx[0].astype(f32)
        self.copy(0, False).wait_recv()
        return total + self.rx[1].astype(f32)

    def sent(self):
        for i in range(4):
            self.sibling(i).wait_send()
        for i in range(3):
            self.copy(i, False).wait_send()


def scatter_scratch():
    part = (ROWS, WIDTH)
    return [
        pltpu.VMEM((4,) + part, bf16),
        pltpu.VMEM((3,) + part, bf16),
        pltpu.VMEM((2,) + part, bf16),
        pltpu.VMEM((2,) + part, bf16),
        pltpu.SemaphoreType.DMA((7,)),
        pltpu.SemaphoreType.DMA((8,)),
    ]


def back_product(left, right):
    return lax.dot_general(
        left, right, (((1,), (1,)), ((), ())), preferred_element_type=f32
    )


def lead_sum(left, right):
    return lax.dot_general(
        left, right, (((0,), (0,)), ((), ())), preferred_element_type=f32
    )


def dot(left, right):
    return jnp.dot(left, right, preferred_element_type=f32)


BLOCK = 2 * ROWS


def block_weights(q, k, begin, z, m, mm, span):
    keys = (z + 1) * BLOCK
    key = lax.broadcasted_iota(jnp.int32, (1, keys), 1)
    key = key // BLOCK * span + key % BLOCK + mm * BLOCK
    token = z * span + m * BLOCK + lax.broadcasted_iota(jnp.int32, (BLOCK, 1), 0)
    e = jnp.exp(back_product(q, k))
    return jnp.where((key >= begin) & (key <= token), e, 0.0)


VM = pltpu.VMEM


def vspecs(n):
    return [pl.BlockSpec(memory_space=VM)] * n


def begin_of(token, doc_ref):
    begin = jnp.zeros(token.shape, jnp.int32)
    start = doc_ref[0, 0]
    for d in range(1, doc_ref.shape[1]):
        begin = jnp.where(token >= start, start, begin)
        start = start + doc_ref[0, d]
    return begin


def turn(v):
    lane = lax.broadcasted_iota(jnp.int32, v.shape, 1)
    n = v.shape[1]
    return jnp.where(lane % 64 < 32, pltpu.roll(v, n - 32, 1), pltpu.roll(v, 32, 1))


def head_scale(v):
    sq = v * v
    if v.shape[1] == 64:
        return lax.rsqrt(jnp.mean(sq, axis=1, keepdims=True) + epsilon)
    low = lax.broadcasted_iota(jnp.int32, v.shape, 1) < 64
    a = jnp.sum(jnp.where(low, sq, 0.0), axis=1, keepdims=True)
    b = jnp.sum(jnp.where(low, 0.0, sq), axis=1, keepdims=True)
    return lax.rsqrt(jnp.where(low, a, b) * (1.0 / 64) + epsilon)


def block_kernel(
    doc_ref, x_ref, c_ref, wh_own, wg_own, wu_own, wd_own, wo_own,
    again_ref, qgain_ref, kgain_ref, fgain_ref,
    out_ref, igrad_ref, gains_ref, heads_ref, attn_ref, gate_ref, up_ref, down_ref,
    x_all, c_all, w_heads, wg_v, wu_v, wd_v, wo_v, q_rows, kv_all, att, summed, totals,
    stacked, normed, cosine, sine,
    att_all, branch, gmid_v, dpart, nffn, hid, gg, gu, mid_b, p_out, gate_tx, gate_rx, down_tx, down_rx,
    up_tx, up_rx, br_own,
    a_sib, a_sum, a_relay, a_rx, s_a, r_a, d_sib, d_sum, d_relay, d_rx, s_d, r_d,
    s_p, r_p,
    g_v, dkv_acc, dkv_rx, gs_v,
    h_tx, h_rx, ap_tx, ap_rx, gn_tx, gn_rx, gt_tx, gt_rx, w_tx, w_rx,
    s_x0, r_x0, s_c, r_c, s_h0, r_h0, s_w0, r_w0, s_v, r_v, s_o, r_o, s_k, r_k, ld,
    s_att, r_att, s_pass, s_sib, r_sib, s_br, r_br, s_x, r_x,
    s_dk, r_dk, s_h, r_h, s_ap, r_ap, s_g, r_g, s_t, r_t, s_w, r_w,
):
    z, m, core, f = who()
    M = lax.axis_size("ctx") // 8
    T = 2 * M
    span = lax.axis_size("ctx") // 4 * ROWS
    each = WIDTH // lax.axis_size("ctx")
    seg = FF // lax.axis_size("ctx")
    half_width = WIDTH // 2
    partner, middle, end, at_end = line_of(z)
    sib = dev(z, m, 1 - core, f)
    zs = [(z + s) % 4 for s in (1, 2, 3)]
    zpeers = [dev(zz, m, core, f) for zz in zs]
    cross = [dev(zz, m, 1 - core, f) for zz in zs]
    hm = m % 2
    pair = dev(z, m, core, 1 - f)
    beside = dev(z, m + 1 - 2 * hm, core, f)
    mpeers = [dev(z, (m + s) % M, core, f) for s in range(1, M)]
    group = m * 2 + f
    others = [(group + s) % T for s in range(1, T)]
    tpeers = [dev(z, o // 2, core, o % 2) for o in others]
    owner = f == z // 2
    me = slot(z, core)

    pieces = [(group + s) % T for s in range(T)]
    rest_to = [core * M + p // 2 for p in pieces]
    piece_to = [dev(z, rr // 2, rr % 2, p % 2) for rr, p in zip(rest_to, pieces)]
    to_self = [(rr == m * 2 + core) & (p % 2 == f) for rr, p in zip(rest_to, pieces)]
    rest = m * 2 + core
    core_from = rest // M
    sources = [(group + s) % T for s in range(T)]
    piece_from = [dev(z, o // 2, core_from, o % 2) for o in sources]
    from_self = [(core_from == core) & (o == group) for o in sources]

    mine = pl.ds(pl.multiple_of(f * half_width, half_width), half_width)
    load_heads = pltpu.make_async_copy(wh_own, w_heads.at[mine], ld.at[0])
    load_out = pltpu.make_async_copy(wo_own, wo_v.at[mine], ld.at[1])
    load_gate = pltpu.make_async_copy(wg_own, wg_v.at[mine], ld.at[2])
    load_up = pltpu.make_async_copy(wu_own, wu_v.at[mine], ld.at[3])
    load_down = pltpu.make_async_copy(wd_own, wd_v, ld.at[4])
    for cp in (load_heads, load_out, load_gate, load_up):
        cp.start()

    @pl.when(owner)
    def _():
        load_down.start()

    bar = pltpu.get_barrier_semaphore()
    fixed = [sib] + zpeers + cross + tpeers
    for p in fixed:
        pl.semaphore_signal(bar, inc=1, device_id=p, device_id_type=MESH)
    for s in range(T):

        @pl.when(jnp.logical_not(from_self[s]))
        def _(s=s):
            pl.semaphore_signal(bar, inc=1, device_id=piece_from[s], device_id_type=MESH)

    place = [(zl, cc) for zl in range(2) for cc in range(2)]
    place_dev = [dev(2 * zl + f, m, cc, z // 2) for zl, cc in place]
    place_self = [owner & (z == 2 * zl + f) & (core == cc) for zl, cc in place]
    place_from = [dev(2 * f + zb, m, cc, z % 2) for zb, cc in place]
    from_me = [owner & (z == 2 * f + zb) & (z % 2 == f) & (core == cc) for zb, cc in place]
    for k in range(4):

        @pl.when(jnp.logical_not(from_me[k]))
        def _(k=k):
            pl.semaphore_signal(bar, inc=1, device_id=place_from[k], device_id_type=MESH)

    pl.semaphore_wait(
        bar,
        len(fixed)
        + T
        + 4
        - jnp.where(core_from == core, 1, 0)
        - jnp.where(owner & (z % 2 == f), 1, 0),
    )

    def lane_block(j):
        return pl.ds(pl.multiple_of(j * 128, 128), 128)

    def front():
        gx = Gather(x_ref, x_all, s_x0, r_x0)
        gc = Gather(c_ref, c_all, s_c, r_c)
        gx.own()
        head_rows = pl.ds(f * half_width, half_width)
        heads_copy = rcopy(wh_own, w_heads.at[head_rows], s_h0.at[0], r_h0.at[0], pair)
        heads_copy.start()

        quarter = half_width // 2
        eighth = half_width // 4
        cols = wd_own.shape[0]

        def w_copy(k, stage):
            src, dst = ((wg_own, wg_v), (wu_own, wu_v), (wd_own, wd_v), (wo_own, wo_v))[k]
            base = 0 if k == 2 else (f if stage == 0 else 1 - f) * half_width
            size = (quarter, quarter, cols // 2, eighth)[k]
            part = hm * 2 + core if k == 3 else hm
            place = dst.at[pl.ds(pl.multiple_of(base + part * size, 8), size)]
            if stage == 0:
                here = src.at[pl.ds(pl.multiple_of(part * size, 8), size)]
                return rcopy(here, place, s_w0.at[k], r_w0.at[k], pair)
            return rcopy(place, place, s_v.at[k], r_v.at[k], beside)

        def out_copy(k):
            part = (hm if k == 0 else 1 - hm) * 2 + core
            base = (1 - f) * half_width
            place = wo_v.at[pl.ds(pl.multiple_of(base + part * eighth, 8), eighth)]
            return rcopy(place, place, s_o.at[k], r_o.at[k], sib)

        w_copy(0, 0).start()
        x_all[me] = x_ref[...]
        c_all[me] = c_ref[...]

        lane = lax.broadcasted_iota(jnp.int32, (1, 128), 1) % 32
        freq = jnp.exp(lane.astype(f32) * (-2.0 / 64 * math.log(rope_base)))
        sign = jnp.where(lax.broadcasted_iota(jnp.int32, (1, 128), 1) % 64 < 32, -1.0, 1.0)

        def tokens_of(zz):
            return zz * span + m * BLOCK + lax.broadcasted_iota(jnp.int32, (BLOCK, 1), 0)

        def table(zz, _):
            rows = pl.ds(pl.multiple_of(zz * BLOCK, BLOCK), BLOCK)
            token = tokens_of(zz)
            place = (token - begin_of(token, doc_ref)).astype(f32)
            angle = place * freq
            cosine[rows, :] = jnp.cos(angle)
            sine[rows, :] = jnp.sin(angle) * sign
            return 0

        lax.fori_loop(0, 4, table, 0)
        for k in (1, 3):
            w_copy(k, 0).start()
        for kind in (0, 1, 2):
            gx.take(kind)
        gc.own()

        @pl.when(owner)
        def _():
            w_copy(2, 0).start()

        heads_copy.wait_recv()

        def kv_copy(b, s):
            rows = pl.ds(pl.multiple_of(b * BLOCK, BLOCK), BLOCK)
            place = kv_all.at[m, rows]
            return rcopy(place, place, s_k.at[b, s], r_k.at[b, s], mpeers[s])

        again = again_ref[...]
        qgain = qgain_ref[...]
        kgain = kgain_ref[...]

        gx.rest()
        load_heads.wait()
        for k in range(2):
            w_copy(k, 0).wait_recv()
            w_copy(k, 1).start()

        def project(b, _):
            rows = pl.ds(pl.multiple_of(b * BLOCK, BLOCK), BLOCK)
            x = jnp.concatenate([x_all[2 * b], x_all[2 * b + 1]], axis=0).astype(f32)
            nb = (
                x * lax.rsqrt(jnp.mean(x * x, axis=-1, keepdims=True) + epsilon) * again
            ).astype(bf16)
            normed[rows, :] = nb
            st = dot(nb, w_heads[...])
            stacked[rows, :] = st
            co = cosine[rows, :]
            si = sine[rows, :]
            q = st[:, :128]
            q = q * head_scale(q) * qgain
            q_rows[rows, :] = ((q * co + turn(q) * si) * HEAD_SIZE ** (-0.5)).astype(bf16)
            kv = st[:, 128:]
            low = lax.broadcasted_iota(jnp.int32, kv.shape, 1) < 64
            k = kv * head_scale(kv) * kgain
            kv_all[m, rows, :] = jnp.where(low, k * co + turn(k) * si, kv).astype(bf16)
            for s in range(M - 1):
                kv_copy(b, s).start()
            return 0

        lax.fori_loop(0, 4, project, 0)

        w_copy(3, 0).wait_recv()
        w_copy(3, 1).start()
        out_copy(0).start()

        @pl.when(at_end == 0)
        def _():
            for kind in (0, 1, 2):
                gc.take(kind)

        summed[...] = jnp.zeros_like(summed)
        totals[...] = jnp.zeros_like(totals)

        def attend(s, _):
            mm = (m + M - s) % M

            @pl.when(s > 0)
            def _():
                for b in range(4):
                    rows = pl.ds(b * BLOCK, BLOCK)
                    place = kv_all.at[mm, rows]
                    rcopy(place, place, s_k.at[b, s - 1], r_k.at[b, s - 1], sib).wait_recv()

            @pl.when((s == 1) & jnp.logical_not(owner))
            def _():
                w_copy(2, 0).wait_recv()
                w_copy(2, 1).start()

            for zz in range(4):
                rows = slice(zz * BLOCK, (zz + 1) * BLOCK)
                keys = (zz + 1) * BLOCK
                begin = begin_of(tokens_of(zz), doc_ref)
                for h in range(2):
                    lanes = slice(h * 64, h * 64 + 64)
                    e = block_weights(
                        q_rows[rows, lanes], kv_all[mm, :keys, :64], begin, zz, m, mm, span
                    )
                    summed[rows, lanes] += dot(e.astype(bf16), kv_all[mm, :keys, 64:])
                    totals[rows, lanes] += jnp.broadcast_to(
                        jnp.sum(e, axis=1, keepdims=True), (BLOCK, 64)
                    )
            return 0

        lax.fori_loop(0, M, attend, 0)
        for b in range(4):
            rows = slice(b * BLOCK, (b + 1) * BLOCK)
            att[b] = (summed[rows, :] / totals[rows, :]).astype(bf16)

        def w_got(k):
            dst = (wg_v, wu_v, wd_v, wo_v)[k]
            base = 0 if k == 2 else (1 - f) * half_width
            size = (quarter, quarter, cols // 2, eighth)[k]
            part = (1 - hm) * 2 + core if k == 3 else 1 - hm
            place = dst.at[pl.ds(pl.multiple_of(base + part * size, 8), size)]
            return rcopy(place, place, s_v.at[k], r_v.at[k], beside)

        def ends_take():
            @pl.when(at_end == 1)
            def _():
                for kind in (0, 1, 2):
                    gc.take(kind)

        def out_ready():
            w_got(3).wait_recv()
            out_copy(1).start()
            load_out.wait()
            for k in range(2):
                out_copy(k).wait_recv()

        def glu_ready():
            for k in range(2):
                w_got(k).wait_recv()
            load_gate.wait()
            load_up.wait()

        def rest_ready():
            gc.rest()

            @pl.when(owner)
            def _():
                load_down.wait()

            @pl.when(jnp.logical_not(owner))
            def _():
                w_got(2).wait_recv()

        def sent():
            heads_copy.wait_send()
            gx.sent()
            gc.sent()
            for k in (0, 1, 3):
                w_copy(k, 0).wait_send()
                w_copy(k, 1).wait_send()

            @pl.when(owner)
            def _():
                w_copy(2, 0).wait_send()

            @pl.when(jnp.logical_not(owner))
            def _():
                w_copy(2, 1).wait_send()

            for k in range(2):
                out_copy(k).wait_send()
            for b in range(4):
                for s in range(M - 1):
                    kv_copy(b, s).wait_send()

        return sent, ends_take, out_ready, glu_ready, rest_ready

    front_sent, ends_take, out_ready, glu_ready, rest_ready = front()

    def feed_forward():
        def lanes(j):
            return pl.ds(pl.multiple_of(j * 128, 128), 128)

        order = [end, middle, partner, z]
        to_partner = [end, middle, z, partner]
        to_middle = [3 * (z // 2), 1 + z // 2, end, middle]
        from_slot = [slot(zz, core) for zz in (partner, middle, end)]
        to_p, to_m = dev(partner, m, core, f), dev(middle, m, core, f)

        def att_copy(k, i):
            if k == 0:
                b = to_partner[i]
                return rcopy(
                    att.at[b], att_all.at[b, :, lanes(me)], s_att.at[0, i], r_att.at[0, i], to_p
                )
            if k == 1:
                b = to_middle[i]
                return rcopy(
                    att.at[b],
                    att_all.at[b, :, lanes(me)],
                    s_att.at[1, i],
                    r_att.at[1 + at_end, i],
                    to_m,
                )
            place = att_all.at[order[i], :, lanes(from_slot[k - 1])]
            return rcopy(place, place, s_pass.at[k - 2, i], r_att.at[k - 1, (0, 1, 3, 2)[i]], to_p)

        def sib_att(k, i):
            b = order[i]
            j = me if k == 3 else from_slot[k]
            src = att.at[b] if k == 3 else att_all.at[b, :, lanes(j)]
            return rcopy(src, att_all.at[b, :, lanes(j)], s_sib.at[k, i], r_sib.at[k, i], sib)

        for i in range(4):
            att_copy(1, i).start()
            att_copy(0, i).start()
            sib_att(3, i).start()
        for b in range(4):
            att_all[b, :, lanes(me)] = att[b]

        def forward(i):
            for k in range(3):
                place = att_all.at[order[i], :, lanes(from_slot[k])]
                rcopy(place, place, s_att.at[0, i], r_att.at[k, i], to_p).wait_recv()
                if k > 0:

                    @pl.when(at_end == 0)
                    def _(k=k):
                        att_copy(k + 1, i).start()

                sib_att(k, i).start()

        ends_take()
        sc = Scatter(p_out, a_sib, a_sum, a_relay, a_rx, s_a, r_a)

        forward(0)
        gain = fgain_ref[...]

        def pair_of(ref, b):
            return jnp.concatenate([ref[2 * b], ref[2 * b + 1]], axis=0)

        for i in range(4):
            b = order[i]
            for k in range(4):
                sib_att(k, i).wait_recv()
            if i == 0:
                out_ready()
            mid = pair_of(x_all, b).astype(f32) + dot(att_all[b], wo_v[...])
            nb = (
                mid * lax.rsqrt(jnp.mean(mid * mid, axis=-1, keepdims=True) + epsilon) * gain
            ).astype(bf16)
            nffn[b] = nb
            if i == 3:
                mid_b[0] = mid[:ROWS]
                mid_b[1] = mid[ROWS:]
            for ii in ((1,), (2, 3), (), ())[i]:
                forward(ii)
            if i == 0:
                glu_ready()
            gate = dot(nb, wg_v[...])
            up = dot(nb, wu_v[...])
            sig = 1.0 / (1.0 + jnp.exp(-gate))
            silu = gate * sig
            hb = (silu * up).astype(bf16)
            hid[b] = hb
            if i == 0:
                rest_ready()
            gh = back_product(pair_of(c_all, b), wd_v[...])
            ggb = (gh * up * (sig * (1.0 + gate * (1.0 - sig)))).astype(bf16)
            gub = (gh * silu).astype(bf16)
            gg[b] = ggb
            gu[b] = gub
            pb = (back_product(ggb, wg_v[...]) + back_product(gub, wu_v[...])).astype(bf16)
            p_out[b, 0] = pb[:ROWS]
            p_out[b, 1] = pb[ROWS:]
            sc.sibling(i).start()
            if i > 0:
                sc.pass_on(i - 1)
            if i > 1:
                sc.relay(i - 2)
            db = dot(hb, wd_v[...]).astype(bf16)
            dpart[b, 0] = db[:ROWS]
            dpart[b, 1] = db[ROWS:]

        def x_copy(which, s):
            tx, rx = ((gate_tx, gate_rx), (down_tx, down_rx), (up_tx, up_rx))[which]
            return rcopy(
                tx.at[others[s]], rx.at[group], s_x.at[which, s], r_x.at[which, s], tpeers[s]
            )

        def send_grads(which):
            tx, rx = ((gate_tx, gate_rx), (down_tx, down_rx), (up_tx, up_rx))[which]
            for s in range(T - 1):
                x_copy(which, s).start()
            rx[group] = tx[group]

        def got_grads(which):
            for s in range(T - 1):
                x_copy(which, s).wait_recv()

        def flat(ref):
            return ref[...].reshape(8 * ROWS, ref.shape[-1])

        def glu_grads(grads, tx):
            prod = lead_sum(flat(grads), flat(nffn)).astype(bf16)
            for mm in range(M):
                for ff in range(2):
                    tx[mm * 2 + ff] = prod[
                        mm * seg : (mm + 1) * seg, ff * half_width : (ff + 1) * half_width
                    ]

        def down_grads():
            prod = lead_sum(flat(c_all), flat(hid))
            for mm in range(M):
                for ff in range(2):
                    down_tx[mm * 2 + ff] = jnp.concatenate(
                        [
                            prod[blk * each : (blk + 1) * each]
                            for zl in range(2)
                            for cc in range(2)
                            for blk in [(2 * zl + ff) * 2 * M + mm * 2 + cc]
                        ],
                        axis=0,
                    ).astype(bf16)

        down_grads()
        send_grads(1)
        glu_grads(gg, gate_tx)
        send_grads(0)

        dy = sc.total()
        mid = mid_b[core]
        r = lax.rsqrt(jnp.mean(mid * mid, axis=-1, keepdims=True) + epsilon)
        gdy = gain * dy
        dv = r * gdy - mid * (r * r * r) * jnp.mean(mid * gdy, axis=-1, keepdims=True)
        gmid = c_ref[...].astype(f32) + dv
        gmid_v[...] = gmid
        ffn_part = jnp.sum(dy * mid * r, axis=0, keepdims=True)
        br_own[...] = gmid.astype(bf16)
        branch[me] = br_own[...]

        gb = Gather(br_own, branch, s_br, r_br)
        gb.own()
        glu_grads(gu, up_tx)
        send_grads(2)
        for kind in (0, 1, 2):
            gb.take(kind)
        gb.rest()

        def sent():
            for i in range(4):
                for k in range(2):
                    att_copy(k, i).wait_send()
                for k in range(4):
                    sib_att(k, i).wait_send()

                @pl.when(at_end == 0)
                def _(i=i):
                    att_copy(2, i).wait_send()
                    att_copy(3, i).wait_send()

            gb.sent()
            for which in range(3):
                for s in range(T - 1):
                    x_copy(which, s).wait_send()

        sc.sent()
        return sent, got_grads, ffn_part

    ffn_sent, got_grads, ffn_part = feed_forward()

    def back():
        sd = Scatter(dpart, d_sib, d_sum, d_relay, d_rx, s_d, r_d)
        sp = Scatter(p_out, a_sib, a_sum, a_relay, a_rx, s_p, r_p)
        for i in range(4):
            sd.sibling(i).start()

        def block_rows(b):
            return pl.ds(pl.multiple_of(b * BLOCK, BLOCK), BLOCK)

        def mixed(b, _):
            rows = block_rows(b)
            br = jnp.concatenate([branch[2 * b], branch[2 * b + 1]], axis=0)
            gm = back_product(br, wo_v[pl.ds(pl.multiple_of(me * 128, 128), 128), :])
            inv = 1.0 / totals[rows, :]
            g_v[rows, :] = (gm * inv).astype(bf16)
            w = gm * summed[rows, :] * (inv * inv)
            low = lax.broadcasted_iota(jnp.int32, w.shape, 1) < 64
            a = jnp.sum(jnp.where(low, w, 0.0), axis=1, keepdims=True)
            c = jnp.sum(jnp.where(low, 0.0, w), axis=1, keepdims=True)
            totals[rows, :] = jnp.where(low, a, c)
            return 0

        lax.fori_loop(0, 4, mixed, 0)
        for i in range(3):
            sd.pass_on(i)

        got_grads(1)
        total = down_rx[0].astype(f32)
        for k in range(1, T):
            total = total + down_rx[k].astype(f32)
        for k in range(4):
            w_tx[k] = total[k * each : (k + 1) * each].astype(bf16)
        here = z % 2 * 2 + core

        def w_copy(k):
            return rcopy(w_tx.at[k], w_rx.at[here], s_w.at[k], r_w.at[here], place_dev[k])

        for k in range(4):

            @pl.when(jnp.logical_not(place_self[k]))
            def _(k=k):
                w_copy(k).start()

            @pl.when(place_self[k])
            def _(k=k):
                w_rx[here] = w_tx[k]

        for i in range(2):
            sd.relay(i)

        summed[...] = jnp.zeros_like(summed)

        def kv_copy(s):
            return rcopy(
                nffn.at[:, :, lane_block(s)], dkv_rx.at[s], s_dk.at[s], r_dk.at[s], mpeers[s]
            )

        def attend(s, _):
            mm = (m + 1 + s) % M
            dkv_acc[...] = jnp.zeros_like(dkv_acc)
            for zz in range(4):
                rows = slice(zz * BLOCK, (zz + 1) * BLOCK)
                keys = (zz + 1) * BLOCK
                token = zz * span + m * BLOCK + lax.broadcasted_iota(jnp.int32, (BLOCK, 1), 0)
                begin = begin_of(token, doc_ref)
                for h in range(2):
                    lanes = slice(h * 64, h * 64 + 64)
                    q = q_rows[rows, lanes]
                    g = g_v[rows, lanes]
                    k = kv_all[mm, :keys, :64]
                    v = kv_all[mm, :keys, 64:]
                    e = block_weights(q, k, begin, zz, m, mm, span)
                    dp = back_product(g, v)
                    ds = (e * (dp - totals[rows, h * 64 : h * 64 + 1])).astype(bf16)
                    summed[rows, lanes] += dot(ds, k)
                    dkv_acc[:keys, :64] += lead_sum(ds, q)
                    dkv_acc[:keys, 64:] += lead_sum(e.astype(bf16), g)

            @pl.when(s < M - 1)
            def _():
                nffn[:, :, lane_block(s)] = dkv_acc[...].astype(bf16).reshape(4, BLOCK, 128)

                for ss in range(M - 1):

                    @pl.when(s == ss)
                    def _(ss=ss):
                        kv_copy(ss).start()

            return 0

        lax.fori_loop(0, M, attend, 0)

        def over_groups(rx):
            total = rx[0].astype(f32)
            for k in range(1, T):
                total = total + rx[k].astype(f32)
            return total

        got_grads(0)
        gate_ref[...] = over_groups(gate_rx)

        strip = jnp.concatenate(
            [branch[j, :, pl.ds(pl.multiple_of(z * 256, 128), 256)] for j in range(8)], axis=0
        )
        strip = jnp.concatenate(
            [
                jnp.where(
                    core == 0,
                    strip[:, 2 * mm * each : (2 * mm + 1) * each],
                    strip[:, (2 * mm + 1) * each : (2 * mm + 2) * each],
                )
                for mm in range(M)
            ],
            axis=1,
        )
        prod = lead_sum(strip, att_all[...].reshape(8 * ROWS, WIDTH))
        for mm in range(M):
            for ff in range(2):
                ap_tx[mm * 2 + ff] = prod[
                    mm * each : (mm + 1) * each, ff * half_width : (ff + 1) * half_width
                ].astype(bf16)

        def a_copy(s):
            return rcopy(ap_tx.at[others[s]], ap_rx.at[group], s_ap.at[s], r_ap.at[s], tpeers[s])

        for s in range(M - 1):
            kv_copy(s).wait_recv()
        for s in range(T - 1):
            a_copy(s).start()
        ap_rx[group] = ap_tx[group]

        qgain = qgain_ref[...]
        kgain = kgain_ref[...]

        def head_mean(v):
            low = lax.broadcasted_iota(jnp.int32, v.shape, 1) < 64
            a = jnp.sum(jnp.where(low, v, 0.0), axis=1, keepdims=True)
            c = jnp.sum(jnp.where(low, 0.0, v), axis=1, keepdims=True)
            return jnp.where(low, a, c) * (1.0 / 64)

        def heads_back(i, carry):
            qg, kg, ag = carry
            b = jnp.where(i == 0, sp.order[0], jnp.where(i == 1, sp.order[1], jnp.where(i == 2, sp.order[2], z)))
            rows = block_rows(b)
            co = cosine[rows, :]
            si = sine[rows, :]

            def through(v, dy, gain):
                dy = dy * co - turn(dy) * si
                r = head_scale(v)
                gdy = gain * dy
                dv = r * gdy - v * (r * r * r) * head_mean(v * gdy)
                return dv, jnp.sum(dy * v * r, axis=0, keepdims=True)

            st = stacked[rows, :]
            dq, qpart = through(st[:, :128], summed[rows, :] * HEAD_SIZE ** (-0.5), qgain)
            dkv = dkv_acc[rows, :]
            for s in range(M - 1):
                dkv = dkv + dkv_rx[s, b].astype(f32)
            dk, kpart = through(st[:, 128:], dkv, kgain)
            low = lax.broadcasted_iota(jnp.int32, dkv.shape, 1) < 64
            gs = jnp.concatenate([dq, jnp.where(low, dk, dkv)], axis=1).astype(bf16)
            gs_v[rows, :] = gs
            pb = back_product(gs, w_heads[...])
            xb = jnp.concatenate([x_all[2 * b], x_all[2 * b + 1]], axis=0).astype(f32)
            rb = lax.rsqrt(jnp.mean(xb * xb, axis=-1, keepdims=True) + epsilon)
            ag = ag + jnp.sum(pb * (xb * rb), axis=0, keepdims=True)
            pb = pb.astype(bf16)
            p_out[b, 0] = pb[:ROWS]
            p_out[b, 1] = pb[ROWS:]
            rcopy(
                p_out.at[b, 1 - core], a_sib.at[i], s_p.at[i], r_p.at[i], sib
            ).start()
            return qg + qpart, kg + kpart, ag

        zero = jnp.zeros((1, 128), f32)
        qg, kg, ag = lax.fori_loop(
            0, 4, heads_back, (zero, zero, jnp.zeros((1, WIDTH), f32))
        )
        for i in range(3):
            sp.pass_on(i)

        def stack(row):
            return jnp.concatenate([row[:, k * 128 : (k + 1) * 128] for k in range(8)], axis=0)

        gn_tx[0:8, :] = stack(ag)
        gn_tx[8:16, :] = stack(ffn_part)
        gn_tx[16:24, :] = jnp.concatenate([qg, kg, jnp.zeros((6, 128), f32)], axis=0)
        gpeers = [sib] + zpeers + cross

        def g_copy(k):
            return rcopy(gn_tx, gn_rx.at[k], s_g.at[k], r_g.at[k], gpeers[k])

        for k in range(7):
            g_copy(k).start()

        prod = lead_sum(gs_v[...], normed[...])
        qw, kw = 128 // M, 64 // M
        for i in range(M):
            piece = jnp.concatenate(
                [
                    prod[i * qw : (i + 1) * qw],
                    prod[128 + i * kw : 128 + (i + 1) * kw],
                    prod[192 + i * kw : 192 + (i + 1) * kw],
                ],
                axis=0,
            ).astype(bf16)
            for ff in range(2):
                h_tx[i * 2 + ff] = piece[:, ff * half_width : (ff + 1) * half_width]

        def h_copy(s):
            return rcopy(
                h_tx.at[pieces[s]], h_rx.at[group], s_h.at[s], r_h.at[group], piece_to[s]
            )

        def h_got(s):
            return rcopy(
                h_tx.at[pieces[s]], h_rx.at[sources[s]], s_h.at[s], r_h.at[sources[s]], piece_from[s]
            )

        for s in range(T):

            @pl.when(to_self[s])
            def _(s=s):
                h_rx[group] = h_tx[pieces[s]]

            @pl.when(jnp.logical_not(to_self[s]))
            def _(s=s):
                h_copy(s).start()

        for i in range(2):
            sp.relay(i)
        gains = gn_tx[...]
        for k in range(7):
            g_copy(k).wait_recv()
        for k in range(7):
            gains = gains + gn_rx[k]
        gt_tx[...] = gains

        def t_copy(s):
            return rcopy(gt_tx, gt_rx.at[s], s_t.at[s], r_t.at[s], tpeers[s])

        for s in range(T - 1):
            t_copy(s).start()


        got_grads(2)
        up_ref[...] = over_groups(up_rx)
        for k in range(4):

            @pl.when(jnp.logical_not(from_me[k]))
            def _(k=k):
                rcopy(w_tx.at[k], w_rx.at[k], s_w.at[k], r_w.at[k], place_from[k]).wait_recv()

        down_ref[...] = jnp.concatenate(
            [
                w_rx[zl * 2 + cc, :, mm * seg : (mm + 1) * seg].astype(f32)
                for zl in range(2)
                for mm in range(M)
                for cc in range(2)
            ],
            axis=1,
        )

        out_ref[...] = mid_b[core] + sd.total()
        dy = sp.total()
        x = x_ref[...].astype(f32)
        r = lax.rsqrt(jnp.mean(x * x, axis=-1, keepdims=True) + epsilon)
        gdy = again_ref[...] * dy
        dv = r * gdy - x * (r * r * r) * jnp.mean(x * gdy, axis=-1, keepdims=True)
        igrad_ref[...] = gmid_v[...] + dv

        for s in range(T):

            @pl.when(jnp.logical_not(from_self[s]))
            def _(s=s):
                h_got(s).wait_recv()

        for s in range(T - 1):
            a_copy(s).wait_recv()
        hsum = h_rx[0].astype(f32)
        asum = ap_rx[0].astype(f32)
        for k in range(1, T):
            hsum = hsum + h_rx[k].astype(f32)
            asum = asum + ap_rx[k].astype(f32)
        heads_ref[...] = hsum
        attn_ref[...] = asum

        for s in range(T - 1):
            t_copy(s).wait_recv()
            gains = gains + gt_rx[s]
        gains_ref[...] = gains

        sd.sent()
        sp.sent()
        for k in range(4):

            @pl.when(jnp.logical_not(place_self[k]))
            def _(k=k):
                w_copy(k).wait_send()

        for s in range(M - 1):
            kv_copy(s).wait_send()
        for s in range(T):

            @pl.when(jnp.logical_not(to_self[s]))
            def _(s=s):
                h_copy(s).wait_send()

        for s in range(T - 1):
            a_copy(s).wait_send()
            t_copy(s).wait_send()
        for k in range(7):
            g_copy(k).wait_send()

    back()
    front_sent()
    ffn_sent()


def block(*args, cid):
    n = lax.axis_size("ctx")
    M, T, seg, each = n // 8, n // 4, FF // n, WIDTH // n
    cols = FF // 8
    tokens = 8 * ROWS
    half_width = WIDTH // 2
    part = (ROWS, WIDTH)
    VS, sem = pltpu.VMEM, pltpu.SemaphoreType.DMA
    shape = jax.ShapeDtypeStruct

    def sems(*shapes):
        return [sem(v) for v in shapes]

    return pl.pallas_call(
        block_kernel,
        out_shape=(
            shape(part, f32),
            shape(part, f32),
            shape((24, 128), f32),
            shape((256 // M, half_width), f32),
            shape((each, half_width), f32),
            shape((seg, half_width), f32),
            shape((seg, half_width), f32),
            shape((each, FF // 2), f32),
        ),
        in_specs=[pl.BlockSpec(memory_space=pltpu.SMEM)] + vspecs(2) + any_specs(5) + vspecs(4),
        out_specs=tuple(vspecs(8)),
        scratch_shapes=[
            VS((8,) + part, bf16),
            VS((8,) + part, bf16),
            VS((WIDTH, 256), bf16),
            VS((WIDTH, cols), bf16),
            VS((WIDTH, cols), bf16),
            VS((cols, WIDTH), bf16),
            VS((WIDTH, WIDTH), bf16),
            VS((tokens, 128), bf16),
            VS((M, tokens, 128), bf16),
            VS((4, BLOCK, 128), bf16),
            VS((tokens, 128), f32),
            VS((tokens, 128), f32),
            VS((tokens, 256), f32),
            VS((tokens, WIDTH), bf16),
            VS((tokens, 128), f32),
            VS((tokens, 128), f32),
            VS((4, BLOCK, WIDTH), bf16),
            VS((8,) + part, bf16),
            VS(part, f32),
            VS((4, 2) + part, bf16),
            VS((4, BLOCK, WIDTH), bf16),
            VS((4, BLOCK, cols), bf16),
            VS((4, BLOCK, cols), bf16),
            VS((4, BLOCK, cols), bf16),
            VS((2,) + part, f32),
            VS((4, 2) + part, bf16),
            VS((T, seg, half_width), bf16),
            VS((T, seg, half_width), bf16),
            *[VS((T, 4 * each, cols), bf16)] * 2,
            VS((T, seg, half_width), bf16),
            VS((T, seg, half_width), bf16),
            VS(part, bf16),
            *scatter_scratch(),
            *scatter_scratch(),
            *scatter_scratch()[4:],
            VS((tokens, 128), bf16),
            VS((tokens, 128), f32),
            VS((M - 1, 4, BLOCK, 128), bf16),
            VS((tokens, 256), bf16),
            *[VS((T, 256 // M, half_width), bf16)] * 2,
            *[VS((T, each, half_width), bf16)] * 2,
            VS((24, 128), f32),
            VS((7, 24, 128), f32),
            VS((24, 128), f32),
            VS((T - 1, 24, 128), f32),
            *[VS((4, each, cols), bf16)] * 2,
            *sems((9,), (7,), (9,), (7,), (1,), (1,), (4,), (4,), (4,), (4,), (2,), (2,)),
            *sems((4, M - 1), (4, M - 1), (5,)),
            *sems((2, 4), (3, 4), (2, 4), (4, 4), (4, 4), (9,), (7,), (3, T - 1), (3, T - 1)),
            *sems((M - 1,), (M - 1,), (T,), (T,), (T - 1,), (T - 1,), (7,), (7,)),
            *sems((T - 1,), (T - 1,), (4,), (4,)),
        ],
        compiler_params=pltpu.CompilerParams(
            collective_id=cid, has_side_effects=True, vmem_limit_bytes=VMEM_LIMIT
        ),
        name="block",
    )(*args)


def finish_kernel(out, igrad, heads, attn, gate, up, down, *refs):
    outs, (s_in, s_out), bufs = refs[:9], refs[16:], refs[9:16]
    qw = heads.shape[0] // 2
    kw = qw // 2
    loads = []
    for k, (a, b) in enumerate(zip((out, igrad, heads, attn, gate, up, down), bufs)):
        cp = pltpu.make_async_copy(a, b, s_in.at[k])
        cp.start()
        loads.append(cp)
    o_out, o_igrad, o_query, o_key, o_value, o_attn, o_gate, o_up, o_down = outs
    b_out, b_igrad, b_heads, b_attn, b_gate, b_up, b_down = bufs
    stores = []
    for k, (load, a, b) in enumerate(
        (
            (4, b_gate, o_gate),
            (5, b_up, o_up),
            (6, b_down, o_down),
            (0, b_out, o_out),
            (1, b_igrad, o_igrad),
            (3, b_attn, o_attn),
            (2, b_heads.at[:qw], o_query),
            (None, b_heads.at[qw : qw + kw], o_key),
            (None, b_heads.at[qw + kw :], o_value),
        )
    ):
        if load is not None:
            loads[load].wait()
        cp = pltpu.make_async_copy(a, b, s_out.at[k])
        cp.start()
        stores.append(cp)
    for cp in stores:
        cp.wait()


def finish(*parts):
    out, igrad, heads, attn, gate, up, down = parts
    qw, kw = heads.shape[0] // 2, heads.shape[0] // 4
    shape = jax.ShapeDtypeStruct
    shapes = [
        out.shape, igrad.shape, (qw, heads.shape[1]), (kw, heads.shape[1]), (kw, heads.shape[1]),
        attn.shape, gate.shape, up.shape, down.shape,
    ]
    return pl.pallas_call(
        finish_kernel,
        out_shape=tuple(shape(v, f32) for v in shapes),
        in_specs=any_specs(7),
        out_specs=tuple(any_specs(9)),
        scratch_shapes=[pltpu.VMEM(v.shape, f32) for v in parts]
        + [pltpu.SemaphoreType.DMA((7,)), pltpu.SemaphoreType.DMA((9,))],
        compiler_params=pltpu.CompilerParams(vmem_limit_bytes=VMEM_LIMIT),
        name="finish",
    )(*parts)


def root_mean_norm(rows, gain):
    return (
        rows * lax.rsqrt(jnp.mean(rows * rows, axis=-1, keepdims=True) + epsilon) * gain
    )


def rotary(rows, cosine, sine):
    halfway = rows.shape[-1] // 2
    leading = rows[..., :halfway]
    trailing = rows[..., halfway:]
    return jnp.concatenate(
        [leading * cosine - trailing * sine, leading * sine + trailing * cosine], axis=-1
    )


SWAP = [(0, 1), (1, 0)]


def halves(f, own, other, axis):
    return jnp.where(
        f == 0,
        jnp.concatenate([own, other], axis=axis),
        jnp.concatenate([other, own], axis=axis),
    )


def local(
    hidden_in,
    doc_lengths,
    attn_gain,
    query_gain,
    key_norm_gain,
    ffn_gain,
    query_proj,
    key_weight,
    value_weight,
    attn_proj,
    gate_proj,
    up_proj,
    down_proj,
    out_cotangent,
):
    n_ctx = lax.axis_size("ctx")
    M = n_ctx // 8
    T = 2 * M
    z, m, core, f = who()
    head = slot(z, core)
    tokens = 8 * ROWS
    span = n_ctx // 4 * ROWS
    segment = FF // n_ctx
    columns = M * segment
    half_width = WIDTH // 2
    each = WIDTH // n_ctx

    heads_own = jnp.concatenate(
        [
            lax.dynamic_slice(query_proj, (0, head * 128), (half_width, 128)),
            lax.dynamic_slice(key_weight, (0, head * 64), (half_width, 64)),
            lax.dynamic_slice(value_weight, (0, head * 64), (half_width, 64)),
        ],
        axis=1,
    ).astype(bf16)
    first = z * (n_ctx // 4) + core
    gate_own, up_own = [
        jnp.concatenate(
            [
                lax.dynamic_slice(w, (0, (first + 2 * mm) * segment), (half_width, segment))
                for mm in range(M)
            ],
            axis=1,
        ).astype(bf16)
        for w in (gate_proj, up_proj)
    ]
    down_own = jnp.concatenate(
        [
            lax.dynamic_slice(
                down_proj, ((first + 2 * mm) * segment - f * (FF // 2), 0), (segment, WIDTH)
            )
            for mm in range(M)
        ],
        axis=0,
    ).astype(bf16)
    out_own = attn_proj.astype(bf16)

    cotangent = out_cotangent[0]
    q_gain = jnp.tile(query_gain, 2)[None]
    k_gain = jnp.concatenate([key_norm_gain, jnp.ones((64,), f32)])[None]
    out, igrad, gains, heads, attn, gate, up, down = block(
        doc_lengths,
        hidden_in[0],
        cotangent,
        heads_own,
        gate_own,
        up_own,
        down_own,
        out_own,
        attn_gain[None],
        q_gain,
        k_gain,
        ffn_gain[None],
        cid=1,
    )
    out, igrad, query, key, value, attn, gate, up, down = finish(
        out, igrad, heads, attn, gate, up, down
    )
    return (
        out[None],
        igrad[None],
        gains[:8].reshape(WIDTH),
        gains[16, :64] + gains[16, 64:],
        gains[17, :64],
        gains[8:16].reshape(WIDTH),
        query.T,
        key.T,
        value.T,
        attn.T,
        gate.T,
        up.T,
        down.T,
    )


def solution(mesh):
    in_specs = (
        P("fsdp", "ctx", None),
        P("fsdp", None),
        P(),
        P(),
        P(),
        P(),
        P("fsdp", None),
        P("fsdp", None),
        P("fsdp", None),
        P("fsdp", None),
        P("fsdp", None),
        P("fsdp", None),
        P("fsdp", None),
        P("fsdp", "ctx", None),
    )
    out_specs = (
        P("fsdp", "ctx", None),
        P("fsdp", "ctx", None),
        P(),
        P(),
        P(),
        P(),
        P("fsdp", "ctx"),
        P("fsdp", "ctx"),
        P("fsdp", "ctx"),
        P("fsdp", "ctx"),
        P("fsdp", "ctx"),
        P("fsdp", "ctx"),
        P("fsdp", "ctx"),
    )
    return jax.shard_map(local, mesh=mesh, in_specs=in_specs, out_specs=out_specs, check_vma=False)
```

profile of v0, /device:TPU:0, one launch (start us, length us, event | category | flops | bytes accessed | tf_op | source)
XLA Modules:
  0.0 207.9 jit_solution(172230843952295791)
XLA Ops:
  0.7 1.2 pad_bitcast_fusion.kgain_ref
  1.9 0.7 tile.2
  2.5 0.6 broadcast_in_dim_tile.3.qgain_ref
  3.1 1.0 dynamic-slice_convert_fusion.8
  4.1 1.2 dynamic-slice_convert_fusion.6
  5.3 0.8 pad_maximum_fusion.3.wh_own
  6.1 2.7 %convert_element_type.2.wo_own = bf16[512,1024]{1,0:T(8,128)(2,1)} convert(f32[512,1024]{1,0:T(8,128)} %param.23) | non-fusion elementwise | flops 524288 | bytes 3145728 | tf_op jit(solution)/shard_map/convert_element_type | solution.py:1306
  8.8 1.8 dynamic-slice_convert_fusion.1
  10.6 1.1 pad_maximum_fusion.wd_own
  11.7 2.8 %dynamic-slice_convert_fusion.3 = (bf16[512,288]{1,0:T(8,128)(2,1)S(1)}, bf16[512,288]{1,0:T(8,128)(2,1)S(1)}, bf16[512,288]{1,0:T(8,128)(2,1)S(1)}, bf16[512,288]{1,0:T(8,128)(2,1)S(1)}) fusion(f32[512,4608]{1,0:T(8,128)} %param.25, s32[]{:T(128)S(6)} %select_n.36, s32[]{:T(128)S(6)} %select_n.37, f32[512,4608]{1,0:T(8,128)} %param.24), kind=kLoop, calls=%fused_computation.4 | loop fusion | bytes 2359304 | tf_op jit(solution)/shard_map/convert.2
  14.5 1.1 pad_maximum_fusion.2.wu_own
  15.6 1.1 pad_maximum_fusion.1.wg_own
  16.6 186.7 %block.1 = (f32[128,1024]{1,0:T(8,128)}, f32[128,1024]{1,0:T(8,128)}, f32[24,128]{1,0:T(8,128)}, f32[128,512]{1,0:T(8,128)}, f32[64,512]{1,0:T(8,128)}, /*index=...) custom-call(s32[1,8]{1,0:T(1,128)} %doc_ref.1, bf16[128,1024]{1,0:T(8,128)(2,1)} %bitcast.23, ...), custom_call_target="tpu_custom_call" | custom-call | tf_op jit(solution)/shard_map/block/pallas_call | solution.py:1096
  203.4 0.0 copy-start
  203.4 3.3 %finish.1 = (f32[128,1024]{1,0:T(8,128)}, f32[128,1024]{1,0:T(8,128)}, f32[64,512]{1,0:T(8,128)}, f32[32,512]{1,0:T(8,128)}, f32[32,512]{1,0:T(8,128)}, /*index=...) custom-call(f32[128,1024]{1,0:T(8,128)} %get-tuple-element.30.out, ...), custom_call_target="tpu_custom_call" | custom-call | tf_op jit(solution)/shard_map/finish/pallas_call | solution.py:1212
  206.7 0.0 copy-done
  206.7 0.6 slice_bitcast_fusion.2
  207.3 0.6 slice_bitcast_fusion
Async XLA Ops:
  203.4 3.3 %copy-start = (f32[24,128]{1,0:T(8,128)S(1)}, f32[24,128]{1,0:T(8,128)}, u32[]{:S(2)}) copy-start(f32[24,128]{1,0:T(8,128)} %get-tuple-element.39) | copy-start | bytes 36868
where the time goes:
time: 208 us
  Pallas kernels  190 us (91%)
  local copies, waits for them, and re-layouts  9.73 us (5%)
  other arithmetic  7.37 us (4%)
    pallas_call x1, Pallas kernels, block(): pl.pallas_call(block_kernel, out_shape=(shape(part, f32), shape(part, f32...  187 us
    another operation x4, local copies, waits for them, and re-layouts  6.71 us

commit v1 on v0

--- a/solution.py
+++ b/solution.py
@@ -263,7 +263,7 @@
 
 
 def block_kernel(
-    doc_ref, x_ref, c_ref, wh_own, wg_own, wu_own, wd_own, wo_own,
+    doc_ref, x_ref, c_ref, q_hbm, k_hbm, v_hbm, gate_hbm, up_hbm, down_hbm, out_hbm,
     again_ref, qgain_ref, kgain_ref, fgain_ref,
     out_ref, igrad_ref, gains_ref, heads_ref, attn_ref, gate_ref, up_ref, down_ref,
     x_all, c_all, w_heads, wg_v, wu_v, wd_v, wo_v, q_rows, kv_all, att, summed, totals,
@@ -299,6 +299,7 @@
     tpeers = [dev(z, o // 2, core, o % 2) for o in others]
     owner = f == z // 2
     me = slot(z, core)
+    head = me
 
     pieces = [(group + s) % T for s in range(T)]
     rest_to = [core * M + p // 2 for p in pieces]
@@ -310,18 +311,117 @@
     piece_from = [dev(z, o // 2, core_from, o % 2) for o in sources]
     from_self = [(core_from == core) & (o == group) for o in sources]
 
-    mine = pl.ds(pl.multiple_of(f * half_width, half_width), half_width)
-    load_heads = pltpu.make_async_copy(wh_own, w_heads.at[mine], ld.at[0])
-    load_out = pltpu.make_async_copy(wo_own, wo_v.at[mine], ld.at[1])
-    load_gate = pltpu.make_async_copy(wg_own, wg_v.at[mine], ld.at[2])
-    load_up = pltpu.make_async_copy(wu_own, wu_v.at[mine], ld.at[3])
-    load_down = pltpu.make_async_copy(wd_own, wd_v, ld.at[4])
-    for cp in (load_heads, load_out, load_gate, load_up):
+    stage = [mid_b.at[0], mid_b.at[1], gmid_v, out_ref, igrad_ref]
+    cols = M * seg
+    wide = -(-(128 - math.gcd(seg, 128) + seg) // 128) * 128
+    in_row = WIDTH // wide
+    bands = -(-M // in_row)
+    high = ROWS // bands
+    first_column = [(z * 2 * M + mm * 2 + core) * seg for mm in range(M)]
+    window = [v // 128 * 128 for v in first_column]
+    window = [v - v // (FF - wide + 128) * 128 for v in window]
+    tall = max(d for d in range(8, ROWS + 1, 8) if seg % d == 0)
+    base = f * half_width
+
+    def ff_chunk(w, dst, r):
+        def parts(buf, i):
+            return [
+                pltpu.make_async_copy(
+                    w.at[pl.ds(r * high, high), pl.ds(pl.multiple_of(window[mm], 128), wide)],
+                    buf.at[pl.ds(mm // in_row * high, high), pl.ds(mm % in_row * wide, wide)],
+                    ld.at[i % 5, mm],
+                )
+                for mm in range(M)
+            ]
+
+        def use(buf):
+            pieces = []
+            for mm in range(M):
+                v = buf[
+                    mm // in_row * high : (mm // in_row + 1) * high,
+                    mm % in_row * wide : (mm % in_row + 1) * wide,
+                ]
+                shift = (wide - (first_column[mm] - window[mm])) % wide
+                pieces.append(pltpu.roll(v, shift, 1)[:, :seg])
+            rows = pl.ds(pl.multiple_of(base + r * high, high), high)
+            dst[rows, :] = jnp.concatenate(pieces, axis=1).astype(bf16)
+
+        return parts, use
+
+    def out_chunk(r):
+        def parts(buf, i):
+            return [pltpu.make_async_copy(out_hbm.at[pl.ds(r * ROWS, ROWS)], buf, ld.at[i % 5, 0])]
+
+        def use(buf):
+            wo_v[pl.ds(pl.multiple_of(base + r * ROWS, ROWS), ROWS), :] = buf[...].astype(bf16)
+
+        return parts, use
+
+    def down_chunk(mm, r):
+        def parts(buf, i):
+            row = pl.multiple_of(first_column[mm] - f * (FF // 2) + r * tall, 8)
+            return [
+                pltpu.make_async_copy(
+                    down_hbm.at[pl.ds(row, tall)], buf.at[pl.ds(0, tall)], ld.at[i % 5, 0]
+                )
+            ]
+
+        def use(buf):
+            at = mm * seg + r * tall
+            wd_v[at : at + tall, :] = buf[:tall, :].astype(bf16)
+
+        return parts, use
+
+    chunks = [ff_chunk(gate_hbm, wg_v, r) for r in range(half_width // high)]
+    chunks += [ff_chunk(up_hbm, wu_v, r) for r in range(half_width // high)]
+    chunks += [out_chunk(r) for r in range(half_width // ROWS)]
+    always = len(chunks)
+    chunks += [down_chunk(mm, r) for mm in range(M) for r in range(seg // tall)]
+
+    def fetch(i):
+        def go():
+            for cp in chunks[i][0](stage[i % 5], i):
+                cp.start()
+
+        if i < always:
+            go()
+        elif i < len(chunks):
+            pl.when(owner)(go)
+
+    def take_in(i):
+        def go():
+            for cp in chunks[i][0](stage[i % 5], i):
+                cp.wait()
+            chunks[i][1](stage[i % 5])
+
+        if i < always:
+            go()
+        else:
+            pl.when(owner)(go)
+        fetch(i + 5)
+
+    half_head = head // 2 * 128
+    head_parts = [
+        pltpu.make_async_copy(
+            q_hbm.at[:, pl.ds(pl.multiple_of(head * 128, 128), 128)],
+            stacked.at[pl.ds(0, half_width), pl.ds(0, 128)],
+            ld.at[5, 0],
+        ),
+        pltpu.make_async_copy(
+            k_hbm.at[:, pl.ds(pl.multiple_of(half_head, 128), 128)],
+            stacked.at[pl.ds(0, half_width), pl.ds(128, 128)],
+            ld.at[6, 0],
+        ),
+        pltpu.make_async_copy(
+            v_hbm.at[:, pl.ds(pl.multiple_of(half_head, 128), 128)],
+            stacked.at[pl.ds(half_width, half_width), pl.ds(0, 128)],
+            ld.at[7, 0],
+        ),
+    ]
+    for cp in head_parts:
         cp.start()
-
-    @pl.when(owner)
-    def _():
-        load_down.start()
+    for i in range(5):
+        fetch(i)
 
     bar = pltpu.get_barrier_semaphore()
     fixed = [sib] + zpeers + cross + tpeers
@@ -361,22 +461,33 @@
         gc = Gather(c_ref, c_all, s_c, r_c)
         gx.own()
         head_rows = pl.ds(f * half_width, half_width)
-        heads_copy = rcopy(wh_own, w_heads.at[head_rows], s_h0.at[0], r_h0.at[0], pair)
+        heads_copy = rcopy(w_heads.at[head_rows], w_heads.at[head_rows], s_h0.at[0], r_h0.at[0], pair)
+        for cp in head_parts:
+            cp.wait()
+
+        def half_of(v):
+            return jnp.where(head % 2 == 0, v[:, :64], v[:, 64:])
+
+        w_heads[head_rows, :] = jnp.concatenate(
+            [
+                stacked[:half_width, :128],
+                half_of(stacked[:half_width, 128:]),
+                half_of(stacked[half_width:, :128]),
+            ],
+            axis=1,
+        ).astype(bf16)
         heads_copy.start()
-
         quarter = half_width // 2
         eighth = half_width // 4
-        cols = wd_own.shape[0]
 
         def w_copy(k, stage):
-            src, dst = ((wg_own, wg_v), (wu_own, wu_v), (wd_own, wd_v), (wo_own, wo_v))[k]
+            dst = (wg_v, wu_v, wd_v, wo_v)[k]
             base = 0 if k == 2 else (f if stage == 0 else 1 - f) * half_width
             size = (quarter, quarter, cols // 2, eighth)[k]
             part = hm * 2 + core if k == 3 else hm
             place = dst.at[pl.ds(pl.multiple_of(base + part * size, 8), size)]
             if stage == 0:
-                here = src.at[pl.ds(pl.multiple_of(part * size, 8), size)]
-                return rcopy(here, place, s_w0.at[k], r_w0.at[k], pair)
+                return rcopy(place, place, s_w0.at[k], r_w0.at[k], pair)
             return rcopy(place, place, s_v.at[k], r_v.at[k], beside)
 
         def out_copy(k):
@@ -385,9 +496,22 @@
             place = wo_v.at[pl.ds(pl.multiple_of(base + part * eighth, 8), eighth)]
             return rcopy(place, place, s_o.at[k], r_o.at[k], sib)
 
-        w_copy(0, 0).start()
         x_all[me] = x_ref[...]
         c_all[me] = c_ref[...]
+        each_ff = half_width // high
+        for i in range(each_ff):
+            take_in(i)
+        w_copy(0, 0).start()
+        gx.take(0)
+        for i in range(each_ff, 2 * each_ff):
+            take_in(i)
+        w_copy(1, 0).start()
+        gx.take(1)
+        for i in range(2 * each_ff, always):
+            take_in(i)
+        w_copy(3, 0).start()
+        gx.take(2)
+        gc.own()
 
         lane = lax.broadcasted_iota(jnp.int32, (1, 128), 1) % 32
         freq = jnp.exp(lane.astype(f32) * (-2.0 / 64 * math.log(rope_base)))
@@ -406,11 +530,8 @@
             return 0
 
         lax.fori_loop(0, 4, table, 0)
-        for k in (1, 3):
-            w_copy(k, 0).start()
-        for kind in (0, 1, 2):
-            gx.take(kind)
-        gc.own()
+        for i in range(always, len(chunks)):
+            take_in(i)
 
         @pl.when(owner)
         def _():
@@ -424,11 +545,10 @@
             return rcopy(place, place, s_k.at[b, s], r_k.at[b, s], mpeers[s])
 
         again = again_ref[...]
-        qgain = qgain_ref[...]
-        kgain = kgain_ref[...]
+        qgain = jnp.concatenate([qgain_ref[...]] * 2, axis=1)
+        kgain = jnp.concatenate([kgain_ref[...], jnp.ones((1, 64), f32)], axis=1)
 
         gx.rest()
-        load_heads.wait()
         for k in range(2):
             w_copy(k, 0).wait_recv()
             w_copy(k, 1).start()
@@ -521,22 +641,15 @@
         def out_ready():
             w_got(3).wait_recv()
             out_copy(1).start()
-            load_out.wait()
             for k in range(2):
                 out_copy(k).wait_recv()
 
         def glu_ready():
             for k in range(2):
                 w_got(k).wait_recv()
-            load_gate.wait()
-            load_up.wait()
 
         def rest_ready():
             gc.rest()
-
-            @pl.when(owner)
-            def _():
-                load_down.wait()
 
             @pl.when(jnp.logical_not(owner))
             def _():
@@ -891,8 +1004,8 @@
             a_copy(s).start()
         ap_rx[group] = ap_tx[group]
 
-        qgain = qgain_ref[...]
-        kgain = kgain_ref[...]
+        qgain = jnp.concatenate([qgain_ref[...]] * 2, axis=1)
+        kgain = jnp.concatenate([kgain_ref[...], jnp.ones((1, 64), f32)], axis=1)
 
         def head_mean(v):
             low = lax.broadcasted_iota(jnp.int32, v.shape, 1) < 64
@@ -1105,7 +1218,7 @@
             shape((seg, half_width), f32),
             shape((each, FF // 2), f32),
         ),
-        in_specs=[pl.BlockSpec(memory_space=pltpu.SMEM)] + vspecs(2) + any_specs(5) + vspecs(4),
+        in_specs=[pl.BlockSpec(memory_space=pltpu.SMEM)] + vspecs(2) + any_specs(7) + vspecs(4),
         out_specs=tuple(vspecs(8)),
         scratch_shapes=[
             VS((8,) + part, bf16),
@@ -1155,7 +1268,7 @@
             VS((T - 1, 24, 128), f32),
             *[VS((4, each, cols), bf16)] * 2,
             *sems((9,), (7,), (9,), (7,), (1,), (1,), (4,), (4,), (4,), (4,), (2,), (2,)),
-            *sems((4, M - 1), (4, M - 1), (5,)),
+            *sems((4, M - 1), (4, M - 1), (8, M)),
             *sems((2, 4), (3, 4), (2, 4), (4, 4), (4, 4), (9,), (7,), (3, T - 1), (3, T - 1)),
             *sems((M - 1,), (M - 1,), (T,), (T,), (T - 1,), (T - 1,), (7,), (7,)),
             *sems((T - 1,), (T - 1,), (4,), (4,)),
@@ -1221,32 +1334,6 @@
     )(*parts)
 
 
-def root_mean_norm(rows, gain):
-    return (
-        rows * lax.rsqrt(jnp.mean(rows * rows, axis=-1, keepdims=True) + epsilon) * gain
-    )
-
-
-def rotary(rows, cosine, sine):
-    halfway = rows.shape[-1] // 2
-    leading = rows[..., :halfway]
-    trailing = rows[..., halfway:]
-    return jnp.concatenate(
-        [leading * cosine - trailing * sine, leading * sine + trailing * cosine], axis=-1
-    )
-
-
-SWAP = [(0, 1), (1, 0)]
-
-
-def halves(f, own, other, axis):
-    return jnp.where(
-        f == 0,
-        jnp.concatenate([own, other], axis=axis),
-        jnp.concatenate([other, own], axis=axis),
-    )
-
-
 def local(
     hidden_in,
     doc_lengths,
@@ -1263,63 +1350,20 @@
     down_proj,
     out_cotangent,
 ):
-    n_ctx = lax.axis_size("ctx")
-    M = n_ctx // 8
-    T = 2 * M
-    z, m, core, f = who()
-    head = slot(z, core)
-    tokens = 8 * ROWS
-    span = n_ctx // 4 * ROWS
-    segment = FF // n_ctx
-    columns = M * segment
-    half_width = WIDTH // 2
-    each = WIDTH // n_ctx
-
-    heads_own = jnp.concatenate(
-        [
-            lax.dynamic_slice(query_proj, (0, head * 128), (half_width, 128)),
-            lax.dynamic_slice(key_weight, (0, head * 64), (half_width, 64)),
-            lax.dynamic_slice(value_weight, (0, head * 64), (half_width, 64)),
-        ],
-        axis=1,
-    ).astype(bf16)
-    first = z * (n_ctx // 4) + core
-    gate_own, up_own = [
-        jnp.concatenate(
-            [
-                lax.dynamic_slice(w, (0, (first + 2 * mm) * segment), (half_width, segment))
-                for mm in range(M)
-            ],
-            axis=1,
-        ).astype(bf16)
-        for w in (gate_proj, up_proj)
-    ]
-    down_own = jnp.concatenate(
-        [
-            lax.dynamic_slice(
-                down_proj, ((first + 2 * mm) * segment - f * (FF // 2), 0), (segment, WIDTH)
-            )
-            for mm in range(M)
-        ],
-        axis=0,
-    ).astype(bf16)
-    out_own = attn_proj.astype(bf16)
-
-    cotangent = out_cotangent[0]
-    q_gain = jnp.tile(query_gain, 2)[None]
-    k_gain = jnp.concatenate([key_norm_gain, jnp.ones((64,), f32)])[None]
     out, igrad, gains, heads, attn, gate, up, down = block(
         doc_lengths,
         hidden_in[0],
-        cotangent,
-        heads_own,
-        gate_own,
-        up_own,
-        down_own,
-        out_own,
+        out_cotangent[0],
+        query_proj,
+        key_weight,
+        value_weight,
+        gate_proj,
+        up_proj,
+        down_proj,
+        attn_proj,
         attn_gain[None],
-        q_gain,
-        k_gain,
+        query_gain[None],
+        key_norm_gain[None],
         ffn_gain[None],
         cid=1,
     )

time: 208 us -> 193 us (0.928)
  local copies, waits for them, and re-layouts: 9.73 us -> 1.28 us
  other arithmetic: 7.37 us -> 1.36 us
    another operation x6 -> x0, local copies, waits for them, and re-layouts: 7.96 us -> none
    concatenate x4 -> x0, other arithmetic: 4.04 us -> none  [the longest x2 2.12 us: local(): jnp.concatenate([lax.dynamic_slice(w, (0, (first + 2 * mm) * segment), (h...]
    convert_element_type x1 -> x0, other arithmetic: 2.75 us -> none  [local(): out_own = attn_proj.astype(bf16)]
where the time goes in v1:
time: 193 us
  Pallas kernels  189 us (98%)
    pallas_call x1, Pallas kernels, block(): pl.pallas_call(block_kernel, out_shape=(shape(part, f32), shape(part, f32...  186 us

profile of v1, /device:TPU:0, one launch (start us, length us, event | category | flops | bytes accessed | tf_op | source)
XLA Modules:
  0.0 192.7 jit_solution(16129089445376230848)
XLA Ops:
  0.7 186.1 %block.1 = (f32[128,1024]{1,0:T(8,128)}, f32[128,1024]{1,0:T(8,128)}, f32[24,128]{1,0:T(8,128)}, f32[128,512]{1,0:T(8,128)}, f32[64,512]{1,0:T(8,128)}, /*index=...) custom-call(s32[1,8]{1,0:T(1,128)} %doc_ref.1, bf16[128,1024]{1,0:T(8,128)(2,1)} %bitcast.23, ...), custom_call_target="tpu_custom_call" | custom-call | tf_op jit(solution)/shard_map/block/pallas_call | solution.py:1209
  186.7 3.3 %finish.1 = (f32[128,1024]{1,0:T(8,128)}, f32[128,1024]{1,0:T(8,128)}, f32[64,512]{1,0:T(8,128)}, f32[32,512]{1,0:T(8,128)}, f32[32,512]{1,0:T(8,128)}, /*index=...) custom-call(f32[128,1024]{1,0:T(8,128)} %get-tuple-element.30.out, ...), custom_call_target="tpu_custom_call" | custom-call | tf_op jit(solution)/shard_map/finish/pallas_call | solution.py:1325
  190.0 1.4 slice_bitcast_fusion.2
  191.4 1.3 slice_bitcast_fusion

commit v2 on v1

--- a/solution.py
+++ b/solution.py
@@ -1280,17 +1280,17 @@
     )(*args)
 
 
-def finish_kernel(out, igrad, heads, attn, gate, up, down, *refs):
-    outs, (s_in, s_out), bufs = refs[:9], refs[16:], refs[9:16]
+def finish_kernel(out, igrad, heads, attn, gate, up, down, gains, *refs):
+    outs, small, bufs, (s_in, s_out) = refs[:9], refs[9:13], refs[13:21], refs[21:]
     qw = heads.shape[0] // 2
     kw = qw // 2
     loads = []
-    for k, (a, b) in enumerate(zip((out, igrad, heads, attn, gate, up, down), bufs)):
+    for k, (a, b) in enumerate(zip((out, igrad, heads, attn, gate, up, down, gains), bufs)):
         cp = pltpu.make_async_copy(a, b, s_in.at[k])
         cp.start()
         loads.append(cp)
     o_out, o_igrad, o_query, o_key, o_value, o_attn, o_gate, o_up, o_down = outs
-    b_out, b_igrad, b_heads, b_attn, b_gate, b_up, b_down = bufs
+    b_out, b_igrad, b_heads, b_attn, b_gate, b_up, b_down, b_gains = bufs
     stores = []
     for k, (load, a, b) in enumerate(
         (
@@ -1310,25 +1310,31 @@
         cp = pltpu.make_async_copy(a, b, s_out.at[k])
         cp.start()
         stores.append(cp)
+    again, fgain, qgain, kgain = small
+    loads[7].wait()
+    again[...] = b_gains[:8, :]
+    fgain[...] = b_gains[8:16, :]
+    qgain[...] = b_gains[16:17, :64] + b_gains[16:17, 64:]
+    kgain[...] = b_gains[17:18, :64]
     for cp in stores:
         cp.wait()
 
 
 def finish(*parts):
-    out, igrad, heads, attn, gate, up, down = parts
+    out, igrad, heads, attn, gate, up, down, _ = parts
     qw, kw = heads.shape[0] // 2, heads.shape[0] // 4
     shape = jax.ShapeDtypeStruct
     shapes = [
         out.shape, igrad.shape, (qw, heads.shape[1]), (kw, heads.shape[1]), (kw, heads.shape[1]),
-        attn.shape, gate.shape, up.shape, down.shape,
+        attn.shape, gate.shape, up.shape, down.shape, (8, 128), (8, 128), (1, 64), (1, 64),
     ]
     return pl.pallas_call(
         finish_kernel,
         out_shape=tuple(shape(v, f32) for v in shapes),
-        in_specs=any_specs(7),
-        out_specs=tuple(any_specs(9)),
+        in_specs=any_specs(8),
+        out_specs=tuple(any_specs(9) + vspecs(4)),
         scratch_shapes=[pltpu.VMEM(v.shape, f32) for v in parts]
-        + [pltpu.SemaphoreType.DMA((7,)), pltpu.SemaphoreType.DMA((9,))],
+        + [pltpu.SemaphoreType.DMA((8,)), pltpu.SemaphoreType.DMA((9,))],
         compiler_params=pltpu.CompilerParams(vmem_limit_bytes=VMEM_LIMIT),
         name="finish",
     )(*parts)
@@ -1367,16 +1373,16 @@
         ffn_gain[None],
         cid=1,
     )
-    out, igrad, query, key, value, attn, gate, up, down = finish(
-        out, igrad, heads, attn, gate, up, down
+    out, igrad, query, key, value, attn, gate, up, down, again, fgain, qgain, kgain = finish(
+        out, igrad, heads, attn, gate, up, down, gains
     )
     return (
         out[None],
         igrad[None],
-        gains[:8].reshape(WIDTH),
-        gains[16, :64] + gains[16, 64:],
-        gains[17, :64],
-        gains[8:16].reshape(WIDTH),
+        again.reshape(WIDTH),
+        qgain.reshape(HEAD_SIZE),
+        kgain.reshape(HEAD_SIZE),
+        fgain.reshape(WIDTH),
         query.T,
         key.T,
         value.T,

time: 193 us -> 191 us (0.990)
  no operation moved by 1% of the time
where the time goes in v2:
time: 191 us
  Pallas kernels  190 us (99%)
    pallas_call x1, Pallas kernels, block(): pl.pallas_call(block_kernel, out_shape=(shape(part, f32), shape(part, f32...  186 us
    pallas_call x1, Pallas kernels, finish(): pl.pallas_call(finish_kernel, out_shape=tuple((shape(v, f32) for v in sha...  3.92 us

profile of v2, /device:TPU:0, one launch (start us, length us, event | category | flops | bytes accessed | tf_op | source)
XLA Modules:
  0.0 190.8 jit_solution(14141049964692451730)
XLA Ops:
  0.7 186.1 %block.1 = (f32[128,1024]{1,0:T(8,128)}, f32[128,1024]{1,0:T(8,128)}, f32[24,128]{1,0:T(8,128)}, f32[128,512]{1,0:T(8,128)}, f32[64,512]{1,0:T(8,128)}, /*index=...) custom-call(s32[1,8]{1,0:T(1,128)} %doc_ref.1, bf16[128,1024]{1,0:T(8,128)(2,1)} %bitcast.19, ...), custom_call_target="tpu_custom_call" | custom-call | tf_op jit(solution)/shard_map/block/pallas_call | solution.py:1209
  186.7 3.9 %finish.1 = (f32[128,1024]{1,0:T(8,128)}, f32[128,1024]{1,0:T(8,128)}, f32[64,512]{1,0:T(8,128)}, f32[32,512]{1,0:T(8,128)}, f32[32,512]{1,0:T(8,128)}, /*index=...) custom-call(f32[128,1024]{1,0:T(8,128)} %get-tuple-element.34.out, ...), custom_call_target="tpu_custom_call" | custom-call | tf_op jit(solution)/shard_map/finish/pallas_call | solution.py:1331
